TPU v7x, 32 devices: a whole 2x2x4 slice. The times are simulated.
32 devices in a mesh: wide: 8 (over z, y), lev: 4 (over x, core).
Axes of the slice: x: 2, y: 2, z: 4, core: 2. Of those that a mesh axis runs over, the one named last changes fastest.
Arguments:
- ensemble: float32 [128, 64, 1024], P(None, 'lev', 'wide'), may hold values from -6 to 6
- innovation: float32 [64, 1024], P('lev', 'wide'), may hold values from -0.4 to 0.4
- obs_inverse: float32 [64, 1024], P('lev', 'wide'), may hold values from 100 to 600
- root_tiles: float32 [8, 128, 128], replicated, may hold values from -0.1875 to 0.1875
- col_index: int32 [8, 8], replicated, may hold values from 0 to 7
- vert_weight: float32 [9, 64], replicated, may hold values from -1 to 1
- member_weight: float32 [128], replicated, may hold values from 0.04 to 0.1
- obs_blocks: int32 [8], replicated, may hold values from 0 to 7
Outputs:
- control: float32 [128, 64, 1024], P(None, 'lev', 'wide')
- increment: float32 [64, 1024], P('lev', 'wide')
Inputs may be any that keep to these rules, and one draw needn't show every extreme that they name: `col_index`: column block numbers; repeats allowed. `obs_blocks`: observed column block numbers; a block listed several times counts that many times.
All inputs are finite; a program needn't handle non-finite values.
Results may differ from a plain program's by a relative error of at most 0.0001.
Values sent between devices are 32-bit elements; how exact they have to be, the bound alone decides.
No kernel may reach another device: no remote copies, remote signals or barrier semaphores. Data moves between devices by JAX's collectives and lax.ppermute only.
A program may use at most 128 MiB of HBM per device.

v0:
```python
import functools

import jax
import jax.numpy as jnp
from jax import lax
from jax.experimental import pallas as pl
from jax.experimental.pallas import tpu as pltpu
from jax.sharding import PartitionSpec as P

TAPS = 9
REACH = 4
ARRIVE = (7, 3, 6, 2, 5, 1, 4)
SPANS = ((0, 4), (6, 8), (4, 6))


def with_halo(block, sides, width):
    for axis, dim in sides:
        count = lax.axis_size(axis)
        forward = [(i, i + 1) for i in range(count - 1)]
        backward = [(target, source) for source, target in forward]
        low = lax.ppermute(
            lax.slice_in_dim(block, block.shape[dim] - width, None, axis=dim), axis, forward
        )
        high = lax.ppermute(lax.slice_in_dim(block, 0, width, axis=dim), axis, backward)
        block = jnp.concatenate([low, block, high], axis=dim)
    return block


def horizontal(values, root_tiles, col_index):
    slot_count, block_size = (root_tiles.shape[0], root_tiles.shape[1])
    members, levels, columns = values.shape
    row_blocks = columns // block_size
    blocks = values.reshape(members, levels, row_blocks, block_size)
    picked = jnp.take(blocks, col_index.reshape(-1), axis=2)
    picked = picked.reshape(members * levels * row_blocks, slot_count * block_size)
    stacked = root_tiles.reshape(slot_count * block_size, block_size)
    product = jnp.dot(
        picked, stacked, precision=lax.Precision.HIGHEST, preferred_element_type=jnp.float32
    )
    return product.reshape(values.shape)


def horizontal_t(values, root_tiles, col_index):
    slot_count, block_size = (root_tiles.shape[0], root_tiles.shape[1])
    members, levels, columns = values.shape
    row_blocks = columns // block_size
    flat = values.reshape(-1, block_size)
    stacked = jnp.transpose(root_tiles, (2, 0, 1)).reshape(block_size, slot_count * block_size)
    product = jnp.dot(
        flat, stacked, precision=lax.Precision.HIGHEST, preferred_element_type=jnp.float32
    )
    product = product.reshape(members, levels, row_blocks * slot_count, block_size)
    summed = jnp.zeros((members, levels, row_blocks, block_size), jnp.float32)
    summed = summed.at[:, :, col_index.reshape(-1), :].add(product)
    return summed.reshape(values.shape)


def general_body(
    ensemble, innovation, obs_inverse, root_tiles, col_index, vert_weight, member_weight, obs_blocks
):
    block_size = root_tiles.shape[1]
    lev_dev = ensemble.shape[1]
    col_dev = ensemble.shape[2]
    wide_count = lax.axis_size("wide")
    first_block = lax.axis_index("wide") * (col_dev // block_size)
    block_ids = first_block + jnp.arange(col_dev // block_size, dtype=jnp.int32)
    counts = jnp.sum((obs_blocks[:, None] == block_ids[None, :]).astype(jnp.float32), axis=0)
    obs_weight = obs_inverse * jnp.repeat(counts, block_size)[None, :]
    padded_weights = jnp.pad(vert_weight, ((0, 0), (4, 4)))
    level_start = lax.axis_index("lev") * lev_dev
    wide_weights = lax.dynamic_slice_in_dim(padded_weights, level_start, lev_dev + 8, 1)
    own_weights = wide_weights[:, 4 : 4 + lev_dev]
    weighted = member_weight[:, None, None] * ensemble

    def grouped(values):
        return values.reshape(wide_count, values.shape[0] // wide_count, lev_dev, col_dev)

    values = lax.all_to_all(
        grouped(weighted * (-(obs_weight * innovation))[None]),
        "wide",
        split_axis=0,
        concat_axis=3,
        tiled=True,
    )[0]
    blended = horizontal_t(values, root_tiles, col_index)
    padded = with_halo(blended, (("lev", 1),), 4)
    summed = jnp.zeros(values.shape, jnp.float32)
    for reverse_offset in range(9):
        lower = 8 - reverse_offset
        summed = (
            summed
            + wide_weights[reverse_offset, lower : lower + lev_dev][None, :, None]
            * padded[:, lower : lower + lev_dev]
        )
    member_fields = summed[None]
    gradient = lax.all_to_all(member_fields[0], "wide", split_axis=2, concat_axis=0, tiled=True)
    control = jnp.zeros_like(gradient)
    increment = jnp.zeros_like(innovation)
    values = lax.all_to_all(grouped(gradient), "wide", split_axis=0, concat_axis=3, tiled=True)[0]
    padded = with_halo(values, (("lev", 1),), 4)
    blended = jnp.zeros(values.shape, jnp.float32)
    for offset in range(9):
        blended = (
            blended + own_weights[offset][None, :, None] * padded[:, offset : offset + lev_dev]
        )
    mapped = horizontal(blended, root_tiles, col_index)[None]
    by_column = lax.all_to_all(mapped[0], "wide", split_axis=2, concat_axis=0, tiled=True)
    image_field = jnp.sum(weighted * by_column, axis=0)
    grad_norm, observed = lax.psum(
        (jnp.sum(gradient * gradient), jnp.sum(obs_weight * image_field * image_field)),
        ("wide", "lev"),
    )
    curvature = grad_norm + observed
    step_size = grad_norm / curvature
    control = control - step_size * gradient
    increment = increment - step_size * image_field
    return (control, increment)


CHAIN = (4, 2, 1)
UNROLL_PAIRS = 8
UNROLL_MEMBERS = 16
UNROLL_SUM = 16
SPREAD_ROOM = 8
PREPARE_ROOM = 16
MEMBER_ROOM = 24
FINISH_ROOM = 8


def split_high_low(values):
    high = values.astype(jnp.bfloat16)
    return high, (values - high.astype(jnp.float32)).astype(jnp.bfloat16)


SCALARS = pl.BlockSpec(memory_space=pltpu.SMEM)
IN_PLACE = pl.BlockSpec(memory_space=pltpu.HBM)
ON_CHIP = pl.BlockSpec(memory_space=pltpu.VMEM)


def in_place(operand):
    return pltpu.with_memory_space_constraint(operand, pltpu.HBM)


def room(mebibytes):
    return pltpu.CompilerParams(vmem_limit_bytes=mebibytes << 20)


def spread_kernel(ens_any, inverse_any, innov_any, seen_any, *refs):
    wide = ens_any.shape[0]
    blocks, (inverse, innov, seen, sems) = refs[:wide], refs[wide:]
    members = ens_any.shape[1]
    place = lax.axis_index("wide")
    small = [
        pltpu.make_async_copy(seen_any, seen, sems.at[wide]),
        pltpu.make_async_copy(inverse_any, inverse, sems.at[wide + 1]),
        pltpu.make_async_copy(innov_any, innov, sems.at[wide + 2]),
    ]
    fetches = [
        pltpu.make_async_copy(
            ens_any.at[place ^ other], blocks[other].at[pl.ds(0, members)], sems.at[other]
        )
        for other in (*ARRIVE, 0)
        if other < wide
    ]
    for fetch in small + fetches:
        fetch.start()
    for fetch in small:
        fetch.wait()
    count = lax.fori_loop(
        0,
        seen.shape[0],
        lambda i, total: total + (seen[i] == place).astype(jnp.int32),
        jnp.int32(0),
    )
    weight = inverse[...] * count.astype(jnp.float32)
    source = -(weight * innov[...])
    for block in blocks:
        block[members] = source
        block[members + 1] = weight
    for fetch in fetches:
        fetch.wait()


def spread(ensemble, obs_inverse, innovation, obs_blocks):
    wide, members, lev_dev, size = ensemble.shape
    block = jax.ShapeDtypeStruct((members + 2, lev_dev, size), jnp.float32)
    return pl.pallas_call(
        spread_kernel,
        out_shape=[block] * wide,
        in_specs=[IN_PLACE] * 4,
        out_specs=[ON_CHIP] * wide,
        scratch_shapes=[
            pltpu.VMEM((lev_dev, size), jnp.float32),
            pltpu.VMEM((lev_dev, size), jnp.float32),
            pltpu.SMEM(obs_blocks.shape, jnp.int32),
            pltpu.SemaphoreType.DMA((wide + 3,)),
        ],
        compiler_params=room(SPREAD_ROOM),
        cost_estimate=pl.CostEstimate(
            flops=0, bytes_accessed=8 * ensemble.size, transcendentals=0
        ),
    )(*map(in_place, (ensemble, obs_inverse, innovation, obs_blocks)))


def prepare_kernel(
    col_any, tiles_any, weight_ref, high_ref, low_ref, taps_ref, root, col_ref, tiles_ref, sems
):
    blocks, slots = col_ref.shape
    size = tiles_ref.shape[1]
    fetches = [
        pltpu.make_async_copy(col_any, col_ref, sems.at[0]),
        pltpu.make_async_copy(tiles_any, tiles_ref, sems.at[1]),
    ]
    for fetch in fetches:
        fetch.start()
    lev_dev = taps_ref.shape[1] - 2 * REACH
    place, level_start = lax.axis_index("wide"), lax.axis_index("lev") * lev_dev
    root[...] = jnp.zeros_like(root)
    for fetch in fetches:
        fetch.wait()

    @pl.loop(0, slots)
    def _(slot):
        tile = tiles_ref[slot]
        for row in range(blocks):
            lanes = pl.ds(pl.multiple_of((row ^ place) * size, size), size)
            root[col_ref[row, slot] ^ place, :, lanes] += tile

    @pl.loop(0, blocks)
    def _(block):
        high, low = split_high_low(root[block])
        start = pl.multiple_of(block * size, size)
        high_ref[pl.ds(start, size), :] = high
        low_ref[pl.ds(start, size), :] = low

    outer = taps_ref.shape[1]
    levels = weight_ref.shape[0] - 4 * REACH
    window = weight_ref[pl.ds(pl.multiple_of(level_start, 8), lev_dev + 4 * REACH), :]
    target = level_start - REACH + lax.broadcasted_iota(jnp.int32, (outer, size), 0)
    inside = (target >= 0) & (target < levels)
    own = window[2 * REACH :]
    for tap in range(TAPS):
        column = pltpu.roll(window, (-tap) % window.shape[0], 0)[:outer] if tap else window[:outer]
        column = column[:, TAPS - 1 - tap : TAPS - tap]
        taps_ref[tap] = jnp.where(inside, jnp.broadcast_to(column, (outer, size)), 0.0)
        taps_ref[TAPS + tap] = jnp.broadcast_to(own[:outer, tap : tap + 1], (outer, size))


def prepare(root_tiles, col_index, vert_weight, lev_dev):
    size = root_tiles.shape[1]
    blocks = col_index.shape[0]
    columns = blocks * size
    outer = lev_dev + 2 * REACH
    weights = jnp.pad(vert_weight.T, ((2 * REACH, 2 * REACH), (0, 128 - TAPS)))
    part = jax.ShapeDtypeStruct((columns, columns), jnp.bfloat16)
    taps = jax.ShapeDtypeStruct((2 * TAPS, outer, size), jnp.float32)
    return pl.pallas_call(
        prepare_kernel,
        out_shape=(part, part, taps),
        in_specs=[IN_PLACE, IN_PLACE, ON_CHIP],
        out_specs=[ON_CHIP] * 3,
        scratch_shapes=[
            pltpu.VMEM((blocks, size, columns), jnp.float32),
            pltpu.SMEM(col_index.shape, jnp.int32),
            pltpu.VMEM(root_tiles.shape, jnp.float32),
            pltpu.SemaphoreType.DMA((2,)),
        ],
        compiler_params=room(PREPARE_ROOM),
        cost_estimate=pl.CostEstimate(
            flops=8 * columns * columns, bytes_accessed=8 * columns * columns, transcendentals=0
        ),
    )(in_place(col_index), in_place(root_tiles), weights)


def vertical(values, taps, first, count):
    rows = values.shape[0]
    total = taps[first, :count] * values[:count]
    for tap in range(1, TAPS):
        total = total + taps[first + tap, :count] * pltpu.roll(values, rows - tap, 0)[:count]
    return total


def three_pass(parts, rows, high, low, contract):
    dims = (((1,), (contract,)), ((), ()))
    both = lax.dot_general(parts[...], high, dims, preferred_element_type=jnp.float32)
    small = lax.dot_general(parts[:rows, :], low, dims, preferred_element_type=jnp.float32)
    return both[:rows] + (both[rows:] + small)


def gradient_kernel(begin, first, weight_ref, taps_ref, high, low, far, near, *refs):
    count = far.shape[0]
    ens, refs = refs[:count], refs[count:]
    if not first:
        sofar, refs = refs[0], refs[1:]
    field, parts, grads = refs[0], refs[-1], refs[1:-1]
    slots, lev_dev, size = ens[0].shape
    members = slots - 2
    columns = high.shape[0]
    outer = lev_dev + 2 * REACH
    rows = members * outer
    first_weight = lax.axis_index("wide") * members
    odd = lax.axis_index("lev") % 2 == 1
    for block in range(count):

        def extended(member):
            one, two = far[block, member], near[block, member]
            below, above = jnp.where(odd, two, one), jnp.where(odd, one, two)
            return jnp.concatenate([below, ens[block][member], above], axis=0)

        source = extended(members)
        lanes = slice(block * size, (block + 1) * size)

        @pl.loop(0, members // 2, unroll=UNROLL_PAIRS)
        def _(pair):
            pieces = []
            for half in range(2):
                member = 2 * pair + half
                product = weight_ref[first_weight + member] * (extended(member) * source)
                pieces.append(vertical(product, taps_ref, 0, outer))
            upper, lower = split_high_low(jnp.concatenate(pieces, axis=0))
            start = pl.multiple_of(pair * 2 * outer, 2 * outer)
            parts[pl.ds(start, 2 * outer), lanes] = upper
            start = pl.multiple_of(rows + pair * 2 * outer, 2 * outer)
            parts[pl.ds(start, 2 * outer), lanes] = lower

    span = slice(begin * size, (begin + count) * size)
    step = min(2 * size, columns)
    for at in range(0, columns, step):
        total = three_pass(parts, rows, high[at : at + step, span], low[at : at + step, span], 1)
        if not first:
            total = total + sofar[:, at : at + step]
        field[:, at : at + step] = total
    for block, grad in enumerate(grads):
        lanes = slice(block * size, (block + 1) * size)
        for member in range(members):
            start = member * outer + REACH
            grad[member] = field[start : start + lev_dev, lanes]


def gradient_part(weights, taps, high, low, halo_pair, arrived, begin, sofar, last):
    slots, lev_dev, size = arrived[0].shape
    members = slots - 2
    columns = high.shape[0]
    rows = members * (lev_dev + 2 * REACH)
    field = jax.ShapeDtypeStruct((rows, columns), jnp.float32)
    grads = [jax.ShapeDtypeStruct((members, lev_dev, size), jnp.float32)] * (columns // size)
    outs = [field] + (grads if last else [])
    operands = [taps, high, low, *halo_pair, *arrived] + ([] if sofar is None else [sofar])
    span = len(arrived) * size
    return pl.pallas_call(
        functools.partial(gradient_kernel, begin, sofar is None),
        out_shape=outs,
        in_specs=[SCALARS] + [ON_CHIP] * len(operands),
        out_specs=[ON_CHIP] * len(outs),
        scratch_shapes=[pltpu.VMEM((2 * rows, span), jnp.bfloat16)],
        compiler_params=room(MEMBER_ROOM),
        cost_estimate=pl.CostEstimate(
            flops=6 * rows * columns * span, bytes_accessed=4 * rows * columns, transcendentals=0
        ),
    )(weights, *operands)


def image_kernel(weight_ref, taps_ref, high, low, field, *refs):
    ens, (image_ref, parts, mapped) = refs[:-3], refs[-3:]
    place = lax.axis_index("wide")
    slots, lev_dev, size = ens[0].shape
    members = slots - 2
    columns = high.shape[0]
    outer = lev_dev + 2 * REACH
    first_weight = lax.axis_index("wide") * members
    rows = members * lev_dev
    norm = jnp.zeros((lev_dev, size), jnp.float32)
    for block in range(len(ens)):
        lanes = slice(block * size, (block + 1) * size)

        def blend(member, norm):
            values = field[pl.ds(pl.multiple_of(member * outer, 8), outer), lanes]
            own = pltpu.roll(values, outer - REACH, 0)[:lev_dev]
            upper, lower = split_high_low(vertical(values, taps_ref, TAPS, lev_dev))
            parts[pl.ds(pl.multiple_of(member * lev_dev, lev_dev), lev_dev), lanes] = upper
            start = pl.multiple_of(rows + member * lev_dev, lev_dev)
            parts[pl.ds(start, lev_dev), lanes] = lower
            return norm + own * own

        norm = lax.fori_loop(0, members, blend, norm, unroll=UNROLL_MEMBERS)
    image_ref[len(ens)] = norm

    step = min(2 * size, columns)
    for at in range(0, columns, step):
        mapped[:, at : at + step] = three_pass(
            parts, rows, high[:, at : at + step], low[:, at : at + step], 0
        )
    for block in range(len(ens)):
        lanes = slice(block * size, (block + 1) * size)

        def add(member, total):
            start = pl.multiple_of(member * lev_dev, lev_dev)
            weighted = weight_ref[first_weight + member] * ens[block][member]
            return total + weighted * mapped[pl.ds(start, lev_dev), lanes]

        image_ref[place ^ block] = lax.fori_loop(
            0, members, add, jnp.zeros((lev_dev, size), jnp.float32), unroll=UNROLL_SUM
        )


def image_part(weights, taps, high, low, field, arrived):
    slots, lev_dev, size = arrived[0].shape
    columns = high.shape[0]
    rows = (slots - 2) * lev_dev
    return pl.pallas_call(
        image_kernel,
        out_shape=jax.ShapeDtypeStruct((len(arrived) + 1, lev_dev, size), jnp.float32),
        in_specs=[SCALARS] + [ON_CHIP] * (4 + len(arrived)),
        out_specs=ON_CHIP,
        scratch_shapes=[
            pltpu.VMEM((2 * rows, columns), jnp.bfloat16),
            pltpu.VMEM((rows, columns), jnp.float32),
        ],
        compiler_params=room(MEMBER_ROOM),
        cost_estimate=pl.CostEstimate(
            flops=6 * rows * columns * columns, bytes_accessed=4 * rows * columns, transcendentals=0
        ),
    )(weights, taps, high, low, field, *arrived)


def observe_kernel(one_ref, two_ref, *refs):
    ens, (image_ref, sums_ref) = refs[:-2], refs[-2:]
    members = ens[0].shape[0] - 2
    place = lax.axis_index("wide")
    total = jnp.zeros(image_ref.shape, jnp.float32)
    for block, ens_ref in enumerate(ens):
        image = one_ref[place ^ block] + two_ref[place ^ block]
        total = total + ens_ref[members + 1] * image * image
        if block == 0:
            image_ref[...] = image
    sums_ref[0] = one_ref[len(ens)] + two_ref[len(ens)]
    sums_ref[1] = total


def observe(one, two, arrived):
    own = one.shape[1:]
    return pl.pallas_call(
        observe_kernel,
        out_shape=[
            jax.ShapeDtypeStruct(own, jnp.float32),
            jax.ShapeDtypeStruct((2, *own), jnp.float32),
        ],
        in_specs=[ON_CHIP] * (2 + len(arrived)),
        out_specs=[ON_CHIP] * 2,
        compiler_params=room(FINISH_ROOM),
    )(one, two, *arrived)


def finish_kernel(image_ref, *refs):
    wide = len(refs) - 6
    one_ref, two_ref, grad_refs, (control_any, increment_ref, scaled, sems) = (
        *refs[:2],
        refs[2 : wide + 2],
        refs[wide + 2 :],
    )
    place = lax.axis_index("wide")
    sums = one_ref[...] + two_ref[...]
    norm = jnp.sum(sums[0], keepdims=True)
    observed = jnp.sum(sums[1], keepdims=True)
    scale = -(norm / (norm + observed))
    increment_ref[...] = scale * image_ref[...]
    stores = []
    for other, grad in enumerate(grad_refs):
        scaled[other] = scale[None] * grad[...]
        stores.append(
            pltpu.make_async_copy(scaled.at[other], control_any.at[place ^ other], sems.at[other])
        )
        stores[-1].start()
    for store in stores:
        store.wait()


def finish(image, one, two, grads):
    wide = len(grads)
    control = jax.ShapeDtypeStruct((wide, *grads[0].shape), jnp.float32)
    return pl.pallas_call(
        finish_kernel,
        out_shape=(control, jax.ShapeDtypeStruct(image.shape, jnp.float32)),
        in_specs=[ON_CHIP] * (3 + wide),
        out_specs=[IN_PLACE, ON_CHIP],
        scratch_shapes=[
            pltpu.VMEM(control.shape, jnp.float32),
            pltpu.SemaphoreType.DMA((wide,)),
        ],
        compiler_params=room(FINISH_ROOM),
    )(image, one, two, *grads)


def swap(values, axes, other):
    count = lax.axis_size(axes)
    return lax.ppermute(values, axes, [(i, i ^ other) for i in range(count)])


def halos(arrived):
    reach = 2 * REACH
    count = lax.axis_size("lev")
    top = arrived[0].shape[1] - reach
    odd = lax.axis_index("lev") % 2
    received = []
    for start, offset in ((1, odd * top), (0, (1 - odd) * top)):
        pairs = [(i, i + 1) for i in range(start, count - 1, 2)]
        pairs += [(i + 1, i) for i in range(start, count - 1, 2)]
        edges = jnp.stack(
            [lax.dynamic_slice_in_dim(block[:-1], offset, reach, axis=1) for block in arrived]
        )
        received.append(lax.ppermute(edges, "lev", pairs))
    return received


def member_body(
    ensemble, innovation, obs_inverse, root_tiles, col_index, vert_weight, member_weight, obs_blocks
):
    wide = lax.axis_size("wide")
    members, lev_dev, size = ensemble.shape
    part = members // wide
    sent = spread(
        ensemble.reshape(wide, part, lev_dev, size), obs_inverse, innovation, obs_blocks
    )
    arrived = [sent[0]] + [None] * (wide - 1)
    for other in ARRIVE:
        if other < wide:
            arrived[other] = swap(sent[other], "wide", other)
    high, low, taps = prepare(root_tiles, col_index, vert_weight, lev_dev)
    results = (None,)
    for number, (begin, end) in enumerate(SPANS):
        group = arrived[begin * wide // 8 : end * wide // 8]
        halo_pair = halos(group)
        results = gradient_part(
            member_weight, taps, high, low, halo_pair, group, begin * wide // 8,
            results[0], number == len(SPANS) - 1,
        )
    field, *grads = results
    for other in range(1, wide):
        grads[other] = swap(grads[other], "wide", other)
    image = image_part(member_weight, taps, high, low, field, arrived)
    other_image = jnp.zeros_like(image)
    for step, other in enumerate(CHAIN):
        if step:
            image = image + other_image
        other_image = swap(image, "wide", other)
    image, sums = observe(image, other_image, arrived)
    step, other, other_sums = len(CHAIN), 1, jnp.zeros_like(sums)
    while other < lax.axis_size("lev"):
        if other > 1:
            sums = sums + other_sums
        other_sums = swap(sums, "lev", other)
        step, other = step + 1, other * 2
    control, increment = finish(image, sums, other_sums, grads)
    return control.reshape(ensemble.shape), increment


def solution(mesh):
    in_specs = (P(None, "lev", "wide"), P("lev", "wide"), P("lev", "wide"), P(), P(), P(), P(), P())
    out_specs = (P(None, "lev", "wide"), P("lev", "wide"))

    def body(*args):
        ensemble, root_tiles = args[0], args[3]
        wide, lev = lax.axis_size("wide"), lax.axis_size("lev")
        members, lev_dev, col_dev = ensemble.shape
        fits = (
            wide & (wide - 1) == 0
            and lev & (lev - 1) == 0
            and wide == 8
            and members % (2 * wide) == 0
            and lev_dev % 16 == 0
            and col_dev == root_tiles.shape[1] == 128
        )
        if not fits:
            return general_body(*args)
        return member_body(*args)

    return jax.shard_map(body, mesh=mesh, in_specs=in_specs, out_specs=out_specs, check_vma=False)
```

profile of v0, /device:TPU:18, one launch (start us, length us, event | category | flops | bytes accessed | tf_op | source)
XLA Modules:
  0.0 97.1 jit_solution(13588808817330461544)
XLA Ops:
  0.6 1.4 %shard_map.96 = (f32[18,16,128]{2,1,0:T(8,128)S(1)}, f32[18,16,128]{2,1,0:T(8,128)S(1)}, f32[18,16,128]{2,1,0:T(8,128)S(1)}, f32[18,16,128]{2,1,0:T(8,128)S(1)},...) custom-call(f32[8,16,16,128]{3,2,1,0:T(8,128)} %bitcast.35, ...), custom_call_target="tpu_custom_call" | custom-call | bytes 2097152 | tf_op jit(solution)/shard_map/pallas_call | solution.py:187
  2.5 3.5 %collective-permute-start.1 = (f32[18,16,128]{2,1,0:T(8,128)S(1)}, f32[18,16,128]{2,1,0:T(8,128)S(1)}, u32[]{:S(2)}, u32[]{:S(2)}) collective-permute-start(f32[18,16,128]{2,1,0:T(8,128)S(1)} %get-tuple-element.30), channel_id=1, source_target_pairs={{0,20},{4,16},{8,28},{12,24},{16,4},{20,0},{24,12},{28,8},{1,21},{... | collective-permute-start | bytes 442376 | tf_op jit(solution)/shard_map/ppermute | solution.py:496
  6.5 1.5 %collective-permute-start.5 = (f32[18,16,128]{2,1,0:T(8,128)S(1)}, f32[18,16,128]{2,1,0:T(8,128)S(1)}, u32[]{:S(2)}, u32[]{:S(2)}) collective-permute-start(f32[18,16,128]{2,1,0:T(8,128)S(1)} %get-tuple-element.32), channel_id=1, source_target_pairs={{0,28},{4,24},{8,20},{12,16},{16,12},{20,8},{24,4},{28,0},{1,29},{... | collective-permute-start | bytes 442376 | tf_op jit(solution)/shard_map/ppermute | solution.py:496
  8.0 1.5 %collective-permute-start.8 = (f32[18,16,128]{2,1,0:T(8,128)S(1)}, f32[18,16,128]{2,1,0:T(8,128)S(1)}, u32[]{:S(2)}, u32[]{:S(2)}) collective-permute-start(f32[18,16,128]{2,1,0:T(8,128)S(1)} %get-tuple-element.34), channel_id=1, source_target_pairs={{0,4},{4,0},{8,12},{12,8},{16,20},{20,16},{24,28},{28,24},{1,5},{5... | collective-permute-start | bytes 442376 | tf_op jit(solution)/shard_map/ppermute | solution.py:496
  9.7 2.7 %shard_map.95 = (bf16[1024,1024]{1,0:T(8,128)(2,1)S(1)}, bf16[1024,1024]{1,0:T(8,128)(2,1)S(1)}, f32[18,24,128]{2,1,0:T(8,128)S(1)}) custom-call(s32[8,8]{1,0:T(8,128)} %col_any.1, f32[8,128,128]{2,1,0:T(8,128)} %tiles_any.1, f32[80,128]{1,0:T(8,128)S(1)} %pad.4.weight_ref), custom_call_target="tpu_custom_call" | custom-call | flops 8388608 | bytes 8388608 | tf_op jit(solution)/shard_map/pallas_call | solution.py:257
  12.4 6.9 %collective-permute-done.refs_0_.refs_4_ = f32[18,16,128]{2,1,0:T(8,128)S(1)} collective-permute-done((f32[18,16,128]{2,1,0:T(8,128)S(1)}, f32[18,16,128]{2,1,0:T(8,128)S(1)}, u32[]{:S(2)}, u32[]{:S(2)}) %collective-permute-start) | collective-permute-done | bytes 147488 | tf_op jit(solution)/shard_map/ppermute | solution.py:496
  19.3 3.5 %collective-permute-start.9 = (f32[18,16,128]{2,1,0:T(8,128)S(1)}, f32[18,16,128]{2,1,0:T(8,128)S(1)}, u32[]{:S(2)}, u32[]{:S(2)}) collective-permute-start(f32[18,16,128]{2,1,0:T(8,128)S(1)} %get-tuple-element.35), channel_id=1, source_target_pairs={{0,8},{4,12},{8,0},{12,4},{16,24},{20,28},{24,16},{28,20},{1,9},{5... | collective-permute-start | bytes 442376 | tf_op jit(solution)/shard_map/ppermute | solution.py:496
  22.9 4.0 %collective-permute-start.10 = (f32[18,16,128]{2,1,0:T(8,128)S(1)}, f32[18,16,128]{2,1,0:T(8,128)S(1)}, u32[]{:S(2)}, u32[]{:S(2)}) collective-permute-start(f32[18,16,128]{2,1,0:T(8,128)S(1)} %get-tuple-element.36), channel_id=1, source_target_pairs={{0,12},{4,8},{8,4},{12,0},{16,28},{20,24},{24,20},{28,16},{1,13},{... | collective-permute-start | bytes 442376 | tf_op jit(solution)/shard_map/ppermute | solution.py:496
  26.9 0.7 collective-permute-done.4.refs_0_.refs_6_
  27.7 2.0 %collective-permute-start.2 = (f32[2,17,8,128]{3,2,1,0:T(8,128)S(1)}, f32[2,17,8,128]{3,2,1,0:T(8,128)S(1)}, u32[]{:S(2)}, u32[]{:S(2)}) collective-permute-start(f32[2,17,8,128]{3,2,1,0:T(8,128)S(1)} %pad_maximum_fusion.2), channel_id=1, source_target_pairs={{1,2},{2,1},{5,6},{6,5},{9,10},{10,9},{13,14},{14,13},{17,18},{18,... | collective-permute-start | bytes 417800 | tf_op jit(solution)/shard_map/ppermute | solution.py:511
  29.7 4.3 %collective-permute-done.5.refs_1_.refs_7_ = f32[18,16,128]{2,1,0:T(8,128)S(1)} collective-permute-done((f32[18,16,128]{2,1,0:T(8,128)S(1)}, f32[18,16,128]{2,1,0:T(8,128)S(1)}, u32[]{:S(2)}, u32[]{:S(2)}) %collective-permute-start.5) | collective-permute-done | bytes 147488 | tf_op jit(solution)/shard_map/ppermute | solution.py:496
  34.3 1.9 %collective-permute-start.11 = (f32[4,17,8,128]{3,2,1,0:T(8,128)S(1)}, f32[4,17,8,128]{3,2,1,0:T(8,128)S(1)}, u32[]{:S(2)}, u32[]{:S(2)}) collective-permute-start(f32[4,17,8,128]{3,2,1,0:T(8,128)S(1)} %pad_maximum_fusion), channel_id=1, source_target_pairs={{1,2},{2,1},{5,6},{6,5},{9,10},{10,9},{13,14},{14,13},{17,18},{18,... | collective-permute-start | bytes 835592 | tf_op jit(solution)/shard_map/ppermute | solution.py:511
  36.3 3.6 %collective-permute-start.6 = (f32[2,17,8,128]{3,2,1,0:T(8,128)S(1)}, f32[2,17,8,128]{3,2,1,0:T(8,128)S(1)}, u32[]{:S(2)}, u32[]{:S(2)}) collective-permute-start(f32[2,17,8,128]{3,2,1,0:T(8,128)S(1)} %pad_maximum_fusion.4), channel_id=1, source_target_pairs={{1,2},{2,1},{5,6},{6,5},{9,10},{10,9},{13,14},{14,13},{17,18},{18,... | collective-permute-start | bytes 417800 | tf_op jit(solution)/shard_map/ppermute | solution.py:511
  40.1 2.0 %collective-permute-done.11.far = f32[4,17,8,128]{3,2,1,0:T(8,128)S(1)} collective-permute-done((f32[4,17,8,128]{3,2,1,0:T(8,128)S(1)}, f32[4,17,8,128]{3,2,1,0:T(8,128)S(1)}, u32[]{:S(2)}, u32[]{:S(2)}) %collective-permute-start.11) | collective-permute-done | bytes 278560 | tf_op jit(solution)/shard_map/ppermute | solution.py:511
  42.2 2.9 %shard_map.97.refs_2_ = f32[384,1024]{1,0:T(8,128)S(1)} custom-call(f32[128]{0:T(128)S(1)} %copy-done, f32[18,24,128]{2,1,0:T(8,128)S(1)} %get-tuple-element.26.taps_ref, bf16[1024,1024]{1,0:T(8,128)(2,1)S(1)} %get-tuple-element.27.high, bf16[1024,1024]{1,0:T(8,128)(2,1)S(1)} %get-tuple-element.28.low, f32[4,17,8,128]{3,2,1,0:T(8,128)S(1)} %collective-permute-done.11.far, ...), custom_call_target="tpu_custom_call" | custom-call | flops 1207959552 | bytes 1572864 | tf_op jit(solution)/shard_map/pallas_call | solution.py:350
  45.0 1.8 %shard_map.98.refs_2_ = f32[384,1024]{1,0:T(8,128)S(1)} custom-call(f32[128]{0:T(128)S(1)} %copy-done, f32[18,24,128]{2,1,0:T(8,128)S(1)} %get-tuple-element.26.taps_ref, bf16[1024,1024]{1,0:T(8,128)(2,1)S(1)} %get-tuple-element.27.high, bf16[1024,1024]{1,0:T(8,128)(2,1)S(1)} %get-tuple-element.28.low, f32[2,17,8,128]{3,2,1,0:T(8,128)S(1)} %collective-permute-done.6.far, ...), custom_call_target="tpu_custom_call" | custom-call | flops 603979776 | bytes 1572864 | tf_op jit(solution)/shard_map/pallas_call | solution.py:350
  46.9 1.9 %shard_map.99 = (f32[384,1024]{1,0:T(8,128)S(1)}, f32[16,16,128]{2,1,0:T(8,128)S(1)}, f32[16,16,128]{2,1,0:T(8,128)S(1)}, f32[16,16,128]{2,1,0:T(8,128)S(1)}, f3...) custom-call(f32[128]{0:T(128)S(1)} %copy-done, ...), custom_call_target="tpu_custom_call" | custom-call | flops 603979776 | bytes 1572864 | tf_op jit(solution)/shard_map/pallas_call | solution.py:350
  48.8 3.5 %shard_map.100 = f32[9,16,128]{2,1,0:T(8,128)S(1)} custom-call(f32[128]{0:T(128)S(1)} %copy-done, f32[18,24,128]{2,1,0:T(8,128)S(1)} %get-tuple-element.26.taps_ref, bf16[1024,1024]{1,0:T(8,128)(2,1)S(1)} %get-tuple-element.27.high, bf16[1024,1024]{1,0:T(8,128)(2,1)S(1)} %get-tuple-element.28.low, f32[384,1024]{1,0:T(8,128)S(1)} %get-tuple-element.37.field, ...), custom_call_target="tpu_custom_call" | custom-call | flops 1610612736 | bytes 1048576 | tf_op jit(solution)/shard_map/pallas_call | solution.py:410
  52.3 5.6 %collective-permute-done.13 = f32[9,16,128]{2,1,0:T(8,128)S(1)} collective-permute-done((f32[9,16,128]{2,1,0:T(8,128)S(1)}, f32[9,16,128]{2,1,0:T(8,128)S(1)}, u32[]{:S(2)}, u32[]{:S(2)}) %collective-permute-start.13) | collective-permute-done | bytes 73760 | tf_op jit(solution)/shard_map/ppermute | solution.py:496
  58.0 1.3 %collective-permute-start.18 = (f32[16,16,128]{2,1,0:T(8,128)S(1)}, f32[16,16,128]{2,1,0:T(8,128)S(1)}, u32[]{:S(2)}, u32[]{:S(2)}) collective-permute-start(f32[16,16,128]{2,1,0:T(8,128)S(1)} %get-tuple-element.41), channel_id=1, source_target_pairs={{0,4},{4,0},{8,12},{12,8},{16,20},{20,16},{24,28},{28,24},{1,5},{5... | collective-permute-start | bytes 393224 | tf_op jit(solution)/shard_map/ppermute | solution.py:496
  59.3 1.9 %collective-permute-start.19 = (f32[16,16,128]{2,1,0:T(8,128)S(1)}, f32[16,16,128]{2,1,0:T(8,128)S(1)}, u32[]{:S(2)}, u32[]{:S(2)}) collective-permute-start(f32[16,16,128]{2,1,0:T(8,128)S(1)} %get-tuple-element.42), channel_id=1, source_target_pairs={{0,8},{4,12},{8,0},{12,4},{16,24},{20,28},{24,16},{28,20},{1,9},{5... | collective-permute-start | bytes 393224 | tf_op jit(solution)/shard_map/ppermute | solution.py:496
  61.2 1.9 %collective-permute-done.14 = f32[9,16,128]{2,1,0:T(8,128)S(1)} collective-permute-done((f32[9,16,128]{2,1,0:T(8,128)S(1)}, f32[9,16,128]{2,1,0:T(8,128)S(1)}, u32[]{:S(2)}, u32[]{:S(2)}) %collective-permute-start.14) | collective-permute-done | bytes 73760 | tf_op jit(solution)/shard_map/ppermute | solution.py:496
  63.1 1.3 %collective-permute-start.15 = (f32[9,16,128]{2,1,0:T(8,128)S(1)}, f32[9,16,128]{2,1,0:T(8,128)S(1)}, u32[]{:S(2)}, u32[]{:S(2)}) collective-permute-start(f32[9,16,128]{2,1,0:T(8,128)S(1)} %add.41.one_ref), channel_id=1, source_target_pairs={{0,4},{4,0},{8,12},{12,8},{16,20},{20,16},{24,28},{28,24},{1,5},{5... | collective-permute-start | bytes 221192 | tf_op jit(solution)/shard_map/ppermute | solution.py:496
  64.4 3.1 %collective-permute-done.15.two_ref = f32[9,16,128]{2,1,0:T(8,128)S(1)} collective-permute-done((f32[9,16,128]{2,1,0:T(8,128)S(1)}, f32[9,16,128]{2,1,0:T(8,128)S(1)}, u32[]{:S(2)}, u32[]{:S(2)}) %collective-permute-start.15) | collective-permute-done | bytes 73760 | tf_op jit(solution)/shard_map/ppermute | solution.py:496
  67.9 1.8 %collective-permute-start.21 = (f32[16,16,128]{2,1,0:T(8,128)S(1)}, f32[16,16,128]{2,1,0:T(8,128)S(1)}, u32[]{:S(2)}, u32[]{:S(2)}) collective-permute-start(f32[16,16,128]{2,1,0:T(8,128)S(1)} %get-tuple-element.44), channel_id=1, source_target_pairs={{0,16},{4,20},{8,24},{12,28},{16,0},{20,4},{24,8},{28,12},{1,17},{... | collective-permute-start | bytes 393224 | tf_op jit(solution)/shard_map/ppermute | solution.py:496
  69.7 1.7 %collective-permute-start.22 = (f32[16,16,128]{2,1,0:T(8,128)S(1)}, f32[16,16,128]{2,1,0:T(8,128)S(1)}, u32[]{:S(2)}, u32[]{:S(2)}) collective-permute-start(f32[16,16,128]{2,1,0:T(8,128)S(1)} %get-tuple-element.45), channel_id=1, source_target_pairs={{0,20},{4,16},{8,28},{12,24},{16,4},{20,0},{24,12},{28,8},{1,21},{... | collective-permute-start | bytes 393224 | tf_op jit(solution)/shard_map/ppermute | solution.py:496
  71.4 2.6 %collective-permute-start.23 = (f32[16,16,128]{2,1,0:T(8,128)S(1)}, f32[16,16,128]{2,1,0:T(8,128)S(1)}, u32[]{:S(2)}, u32[]{:S(2)}) collective-permute-start(f32[16,16,128]{2,1,0:T(8,128)S(1)} %get-tuple-element.46), channel_id=1, source_target_pairs={{0,24},{4,28},{8,16},{12,20},{16,8},{20,12},{24,0},{28,4},{1,25},{... | collective-permute-start | bytes 393224 | tf_op jit(solution)/shard_map/ppermute | solution.py:496
  75.0 1.8 %collective-permute-done.21.refs_6_ = f32[16,16,128]{2,1,0:T(8,128)S(1)} collective-permute-done((f32[16,16,128]{2,1,0:T(8,128)S(1)}, f32[16,16,128]{2,1,0:T(8,128)S(1)}, u32[]{:S(2)}, u32[]{:S(2)}) %collective-permute-start.21) | collective-permute-done | bytes 131104 | tf_op jit(solution)/shard_map/ppermute | solution.py:496
  76.8 10.8 %collective-permute-done.22.refs_7_ = f32[16,16,128]{2,1,0:T(8,128)S(1)} collective-permute-done((f32[16,16,128]{2,1,0:T(8,128)S(1)}, f32[16,16,128]{2,1,0:T(8,128)S(1)}, u32[]{:S(2)}, u32[]{:S(2)}) %collective-permute-start.22) | collective-permute-done | bytes 131104 | tf_op jit(solution)/shard_map/ppermute | solution.py:496
  87.6 5.4 %collective-permute-done.23.refs_8_ = f32[16,16,128]{2,1,0:T(8,128)S(1)} collective-permute-done((f32[16,16,128]{2,1,0:T(8,128)S(1)}, f32[16,16,128]{2,1,0:T(8,128)S(1)}, u32[]{:S(2)}, u32[]{:S(2)}) %collective-permute-start.23) | collective-permute-done | bytes 131104 | tf_op jit(solution)/shard_map/ppermute | solution.py:496
  93.0 2.2 %collective-permute-done.24.refs_9_ = f32[16,16,128]{2,1,0:T(8,128)S(1)} collective-permute-done((f32[16,16,128]{2,1,0:T(8,128)S(1)}, f32[16,16,128]{2,1,0:T(8,128)S(1)}, u32[]{:S(2)}, u32[]{:S(2)}) %collective-permute-start.24) | collective-permute-done | bytes 131104 | tf_op jit(solution)/shard_map/ppermute | solution.py:496
  95.3 1.8 %shard_map.102 = (f32[8,16,16,128]{3,2,1,0:T(8,128)}, f32[16,128]{1,0:T(8,128)}) custom-call(f32[16,128]{1,0:T(8,128)S(1)} %get-tuple-element.38.image_ref, f32[2,16,128]{2,1,0:T(8,128)S(1)} %add.42.refs_0_, f32[2,16,128]{2,1,0:T(8,128)S(1)} %collective-permute-done.17.refs_1_, f32[16,16,128]{2,1,0:T(8,128)S(1)} %get-tuple-element.40.refs_2_, ...), custom_call_target="tpu_custom_call" | custom-call | tf_op jit(solution)/shard_map/pallas_call | solution.py:481
  (57 shorter events, 3.0 us)
Async XLA Ops:
  0.6 8.9 %copy-start.1 = (f32[9,64]{1,0:T(8,128)S(1)}, f32[9,64]{1,0:T(8,128)}, u32[]{:S(2)}) copy-start(f32[9,64]{1,0:T(8,128)} %param.13) | copy-start | bytes 6916
  2.1 17.3 %collective-permute-start = (f32[18,16,128]{2,1,0:T(8,128)S(1)}, f32[18,16,128]{2,1,0:T(8,128)S(1)}, u32[]{:S(2)}, u32[]{:S(2)}) collective-permute-start(f32[18,16,128]{2,1,0:T(8,128)S(1)} %get-tuple-element.29), channel_id=1, source_target_pairs={{0,16},{4,20},{8,24},{12,28},{16,0},{20,4},{24,8},{28,12},{1,17},{... | collective-permute-start | bytes 442376 | tf_op jit(solution)/shard_map/ppermute | solution.py:496
  2.5 20.4 %collective-permute-start.1 = (f32[18,16,128]{2,1,0:T(8,128)S(1)}, f32[18,16,128]{2,1,0:T(8,128)S(1)}, u32[]{:S(2)}, u32[]{:S(2)}) collective-permute-start(f32[18,16,128]{2,1,0:T(8,128)S(1)} %get-tuple-element.30), channel_id=1, source_target_pairs={{0,20},{4,16},{8,28},{12,24},{16,4},{20,0},{24,12},{28,8},{1,21},{... | collective-permute-start | bytes 442376 | tf_op jit(solution)/shard_map/ppermute | solution.py:496
  6.0 21.7 %collective-permute-start.4 = (f32[18,16,128]{2,1,0:T(8,128)S(1)}, f32[18,16,128]{2,1,0:T(8,128)S(1)}, u32[]{:S(2)}, u32[]{:S(2)}) collective-permute-start(f32[18,16,128]{2,1,0:T(8,128)S(1)} %get-tuple-element.31), channel_id=1, source_target_pairs={{0,24},{4,28},{8,16},{12,20},{16,8},{20,12},{24,0},{28,4},{1,25},{... | collective-permute-start | bytes 442376 | tf_op jit(solution)/shard_map/ppermute | solution.py:496
  6.5 27.6 %collective-permute-start.5 = (f32[18,16,128]{2,1,0:T(8,128)S(1)}, f32[18,16,128]{2,1,0:T(8,128)S(1)}, u32[]{:S(2)}, u32[]{:S(2)}) collective-permute-start(f32[18,16,128]{2,1,0:T(8,128)S(1)} %get-tuple-element.32), channel_id=1, source_target_pairs={{0,28},{4,24},{8,20},{12,16},{16,12},{20,8},{24,4},{28,0},{1,29},{... | collective-permute-start | bytes 442376 | tf_op jit(solution)/shard_map/ppermute | solution.py:496
  8.0 26.1 %collective-permute-start.8 = (f32[18,16,128]{2,1,0:T(8,128)S(1)}, f32[18,16,128]{2,1,0:T(8,128)S(1)}, u32[]{:S(2)}, u32[]{:S(2)}) collective-permute-start(f32[18,16,128]{2,1,0:T(8,128)S(1)} %get-tuple-element.34), channel_id=1, source_target_pairs={{0,4},{4,0},{8,12},{12,8},{16,20},{20,16},{24,28},{28,24},{1,5},{5... | collective-permute-start | bytes 442376 | tf_op jit(solution)/shard_map/ppermute | solution.py:496
  19.3 14.8 %collective-permute-start.9 = (f32[18,16,128]{2,1,0:T(8,128)S(1)}, f32[18,16,128]{2,1,0:T(8,128)S(1)}, u32[]{:S(2)}, u32[]{:S(2)}) collective-permute-start(f32[18,16,128]{2,1,0:T(8,128)S(1)} %get-tuple-element.35), channel_id=1, source_target_pairs={{0,8},{4,12},{8,0},{12,4},{16,24},{20,28},{24,16},{28,20},{1,9},{5... | collective-permute-start | bytes 442376 | tf_op jit(solution)/shard_map/ppermute | solution.py:496
  22.9 11.3 %collective-permute-start.10 = (f32[18,16,128]{2,1,0:T(8,128)S(1)}, f32[18,16,128]{2,1,0:T(8,128)S(1)}, u32[]{:S(2)}, u32[]{:S(2)}) collective-permute-start(f32[18,16,128]{2,1,0:T(8,128)S(1)} %get-tuple-element.36), channel_id=1, source_target_pairs={{0,12},{4,8},{8,4},{12,0},{16,28},{20,24},{24,20},{28,16},{1,13},{... | collective-permute-start | bytes 442376 | tf_op jit(solution)/shard_map/ppermute | solution.py:496
  27.7 19.2 %collective-permute-start.2 = (f32[2,17,8,128]{3,2,1,0:T(8,128)S(1)}, f32[2,17,8,128]{3,2,1,0:T(8,128)S(1)}, u32[]{:S(2)}, u32[]{:S(2)}) collective-permute-start(f32[2,17,8,128]{3,2,1,0:T(8,128)S(1)} %pad_maximum_fusion.2), channel_id=1, source_target_pairs={{1,2},{2,1},{5,6},{6,5},{9,10},{10,9},{13,14},{14,13},{17,18},{18,... | collective-permute-start | bytes 417800 | tf_op jit(solution)/shard_map/ppermute | solution.py:511
  34.1 8.0 %copy-start = (f32[128]{0:T(128)S(1)}, f32[128]{0:T(128)}, u32[]{:S(2)}) copy-start(f32[128]{0:T(128)} %weight_ref.7) | copy-start | bytes 1540
  34.3 7.9 %collective-permute-start.11 = (f32[4,17,8,128]{3,2,1,0:T(8,128)S(1)}, f32[4,17,8,128]{3,2,1,0:T(8,128)S(1)}, u32[]{:S(2)}, u32[]{:S(2)}) collective-permute-start(f32[4,17,8,128]{3,2,1,0:T(8,128)S(1)} %pad_maximum_fusion), channel_id=1, source_target_pairs={{1,2},{2,1},{5,6},{6,5},{9,10},{10,9},{13,14},{14,13},{17,18},{18,... | collective-permute-start | bytes 835592 | tf_op jit(solution)/shard_map/ppermute | solution.py:511
  36.2 5.9 %collective-permute-start.12 = (f32[4,17,8,128]{3,2,1,0:T(8,128)S(1)}, f32[4,17,8,128]{3,2,1,0:T(8,128)S(1)}, u32[]{:S(2)}, u32[]{:S(2)}) collective-permute-start(f32[4,17,8,128]{3,2,1,0:T(8,128)S(1)} %pad_maximum_fusion.1), channel_id=1, source_target_pairs={{0,1},{2,3},{1,0},{3,2},{4,5},{6,7},{5,4},{7,6},{8,9},{10,11},{9,8... | collective-permute-start | bytes 835592 | tf_op jit(solution)/shard_map/ppermute | solution.py:511
  36.3 8.7 %collective-permute-start.6 = (f32[2,17,8,128]{3,2,1,0:T(8,128)S(1)}, f32[2,17,8,128]{3,2,1,0:T(8,128)S(1)}, u32[]{:S(2)}, u32[]{:S(2)}) collective-permute-start(f32[2,17,8,128]{3,2,1,0:T(8,128)S(1)} %pad_maximum_fusion.4), channel_id=1, source_target_pairs={{1,2},{2,1},{5,6},{6,5},{9,10},{10,9},{13,14},{14,13},{17,18},{18,... | collective-permute-start | bytes 417800 | tf_op jit(solution)/shard_map/ppermute | solution.py:511
  40.0 5.0 %collective-permute-start.7 = (f32[2,17,8,128]{3,2,1,0:T(8,128)S(1)}, f32[2,17,8,128]{3,2,1,0:T(8,128)S(1)}, u32[]{:S(2)}, u32[]{:S(2)}) collective-permute-start(f32[2,17,8,128]{3,2,1,0:T(8,128)S(1)} %pad_maximum_fusion.5), channel_id=1, source_target_pairs={{0,1},{2,3},{1,0},{3,2},{4,5},{6,7},{5,4},{7,6},{8,9},{10,11},{9,8... | collective-permute-start | bytes 417800 | tf_op jit(solution)/shard_map/ppermute | solution.py:511
  42.1 4.7 %collective-permute-start.3 = (f32[2,17,8,128]{3,2,1,0:T(8,128)S(1)}, f32[2,17,8,128]{3,2,1,0:T(8,128)S(1)}, u32[]{:S(2)}, u32[]{:S(2)}) collective-permute-start(f32[2,17,8,128]{3,2,1,0:T(8,128)S(1)} %pad_maximum_fusion.3), channel_id=1, source_target_pairs={{0,1},{2,3},{1,0},{3,2},{4,5},{6,7},{5,4},{7,6},{8,9},{10,11},{9,8... | collective-permute-start | bytes 417800 | tf_op jit(solution)/shard_map/ppermute | solution.py:511
  52.3 5.6 %collective-permute-start.13 = (f32[9,16,128]{2,1,0:T(8,128)S(1)}, f32[9,16,128]{2,1,0:T(8,128)S(1)}, u32[]{:S(2)}, u32[]{:S(2)}) collective-permute-start(f32[9,16,128]{2,1,0:T(8,128)S(1)} %shard_map.100), channel_id=1, source_target_pairs={{0,16},{4,20},{8,24},{12,28},{16,0},{20,4},{24,8},{28,12},{1,17},{... | collective-permute-start | bytes 221192 | tf_op jit(solution)/shard_map/ppermute | solution.py:496
  57.9 5.2 %collective-permute-start.14 = (f32[9,16,128]{2,1,0:T(8,128)S(1)}, f32[9,16,128]{2,1,0:T(8,128)S(1)}, u32[]{:S(2)}, u32[]{:S(2)}) collective-permute-start(f32[9,16,128]{2,1,0:T(8,128)S(1)} %add.40), channel_id=1, source_target_pairs={{0,8},{4,12},{8,0},{12,4},{16,24},{20,28},{24,16},{28,20},{1,9},{5... | collective-permute-start | bytes 221192 | tf_op jit(solution)/shard_map/ppermute | solution.py:496
  58.0 11.7 %collective-permute-start.18 = (f32[16,16,128]{2,1,0:T(8,128)S(1)}, f32[16,16,128]{2,1,0:T(8,128)S(1)}, u32[]{:S(2)}, u32[]{:S(2)}) collective-permute-start(f32[16,16,128]{2,1,0:T(8,128)S(1)} %get-tuple-element.41), channel_id=1, source_target_pairs={{0,4},{4,0},{8,12},{12,8},{16,20},{20,16},{24,28},{28,24},{1,5},{5... | collective-permute-start | bytes 393224 | tf_op jit(solution)/shard_map/ppermute | solution.py:496
  59.3 12.1 %collective-permute-start.19 = (f32[16,16,128]{2,1,0:T(8,128)S(1)}, f32[16,16,128]{2,1,0:T(8,128)S(1)}, u32[]{:S(2)}, u32[]{:S(2)}) collective-permute-start(f32[16,16,128]{2,1,0:T(8,128)S(1)} %get-tuple-element.42), channel_id=1, source_target_pairs={{0,8},{4,12},{8,0},{12,4},{16,24},{20,28},{24,16},{28,20},{1,9},{5... | collective-permute-start | bytes 393224 | tf_op jit(solution)/shard_map/ppermute | solution.py:496
  63.1 4.4 %collective-permute-start.15 = (f32[9,16,128]{2,1,0:T(8,128)S(1)}, f32[9,16,128]{2,1,0:T(8,128)S(1)}, u32[]{:S(2)}, u32[]{:S(2)}) collective-permute-start(f32[9,16,128]{2,1,0:T(8,128)S(1)} %add.41.one_ref), channel_id=1, source_target_pairs={{0,4},{4,0},{8,12},{12,8},{16,20},{20,16},{24,28},{28,24},{1,5},{5... | collective-permute-start | bytes 221192 | tf_op jit(solution)/shard_map/ppermute | solution.py:496
  67.6 6.4 %collective-permute-start.16 = (f32[2,16,128]{2,1,0:T(8,128)S(1)}, f32[2,16,128]{2,1,0:T(8,128)S(1)}, u32[]{:S(2)}, u32[]{:S(2)}) collective-permute-start(f32[2,16,128]{2,1,0:T(8,128)S(1)} %get-tuple-element.39), channel_id=1, source_target_pairs={{0,1},{1,0},{2,3},{3,2},{4,5},{5,4},{6,7},{7,6},{8,9},{9,8},{10,11... | collective-permute-start | bytes 49160 | tf_op jit(solution)/shard_map/ppermute | solution.py:496
  67.6 7.3 %collective-permute-start.20 = (f32[16,16,128]{2,1,0:T(8,128)S(1)}, f32[16,16,128]{2,1,0:T(8,128)S(1)}, u32[]{:S(2)}, u32[]{:S(2)}) collective-permute-start(f32[16,16,128]{2,1,0:T(8,128)S(1)} %get-tuple-element.43), channel_id=1, source_target_pairs={{0,12},{4,8},{8,4},{12,0},{16,28},{20,24},{24,20},{28,16},{1,13},{... | collective-permute-start | bytes 393224 | tf_op jit(solution)/shard_map/ppermute | solution.py:496
  67.9 8.9 %collective-permute-start.21 = (f32[16,16,128]{2,1,0:T(8,128)S(1)}, f32[16,16,128]{2,1,0:T(8,128)S(1)}, u32[]{:S(2)}, u32[]{:S(2)}) collective-permute-start(f32[16,16,128]{2,1,0:T(8,128)S(1)} %get-tuple-element.44), channel_id=1, source_target_pairs={{0,16},{4,20},{8,24},{12,28},{16,0},{20,4},{24,8},{28,12},{1,17},{... | collective-permute-start | bytes 393224 | tf_op jit(solution)/shard_map/ppermute | solution.py:496
  69.7 18.0 %collective-permute-start.22 = (f32[16,16,128]{2,1,0:T(8,128)S(1)}, f32[16,16,128]{2,1,0:T(8,128)S(1)}, u32[]{:S(2)}, u32[]{:S(2)}) collective-permute-start(f32[16,16,128]{2,1,0:T(8,128)S(1)} %get-tuple-element.45), channel_id=1, source_target_pairs={{0,20},{4,16},{8,28},{12,24},{16,4},{20,0},{24,12},{28,8},{1,21},{... | collective-permute-start | bytes 393224 | tf_op jit(solution)/shard_map/ppermute | solution.py:496
  71.4 21.7 %collective-permute-start.23 = (f32[16,16,128]{2,1,0:T(8,128)S(1)}, f32[16,16,128]{2,1,0:T(8,128)S(1)}, u32[]{:S(2)}, u32[]{:S(2)}) collective-permute-start(f32[16,16,128]{2,1,0:T(8,128)S(1)} %get-tuple-element.46), channel_id=1, source_target_pairs={{0,24},{4,28},{8,16},{12,20},{16,8},{20,12},{24,0},{28,4},{1,25},{... | collective-permute-start | bytes 393224 | tf_op jit(solution)/shard_map/ppermute | solution.py:496
  74.0 21.3 %collective-permute-start.24 = (f32[16,16,128]{2,1,0:T(8,128)S(1)}, f32[16,16,128]{2,1,0:T(8,128)S(1)}, u32[]{:S(2)}, u32[]{:S(2)}) collective-permute-start(f32[16,16,128]{2,1,0:T(8,128)S(1)} %get-tuple-element.47), channel_id=1, source_target_pairs={{0,28},{4,24},{8,20},{12,16},{16,12},{20,8},{24,4},{28,0},{1,29},{... | collective-permute-start | bytes 393224 | tf_op jit(solution)/shard_map/ppermute | solution.py:496
  75.0 20.3 %collective-permute-start.17 = (f32[2,16,128]{2,1,0:T(8,128)S(1)}, f32[2,16,128]{2,1,0:T(8,128)S(1)}, u32[]{:S(2)}, u32[]{:S(2)}) collective-permute-start(f32[2,16,128]{2,1,0:T(8,128)S(1)} %add.42.refs_0_), channel_id=1, source_target_pairs={{0,2},{1,3},{2,0},{3,1},{4,6},{5,7},{6,4},{7,5},{8,10},{9,11},{10,... | collective-permute-start | bytes 49160 | tf_op jit(solution)/shard_map/ppermute | solution.py:496
where the time goes:
time: 97.3 us; the launch traced here: 97.1 us
  waiting for transfers between devices  45.6 us (47%)
  starting transfers between devices  34 us (35%)
  Pallas kernels  15.9 us (16%)
  between operations  1 us (1%)
    ppermute x19, waiting for transfers between devices, swap(): return lax.ppermute(values, axes, [(i, i ^ other) for i in range(count)])  43.5 us
    ppermute x19, starting transfers between devices, swap(): return lax.ppermute(values, axes, [(i, i ^ other) for i in range(count)])  26.4 us
    ppermute x6, starting transfers between devices, halos(): received.append(lax.ppermute(edges, 'lev', pairs))  7.66 us
    pallas_call x3, Pallas kernels, gradient_part(): pl.pallas_call(functools.partial(gradient_kernel, begin, sofar is None),...  6.56 us
    pallas_call x1, Pallas kernels, image_part(): pl.pallas_call(image_kernel, out_shape=jax.ShapeDtypeStruct((len(arrived)...  3.47 us
    pallas_call x1, Pallas kernels, prepare(): pl.pallas_call(prepare_kernel, out_shape=(part, part, taps), in_specs=[IN...  2.73 us
    ppermute x6, waiting for transfers between devices, halos(): received.append(lax.ppermute(edges, 'lev', pairs))  2.06 us
  transfers between devices with their start and end apart: 25, of which 12 were waited for; matrix products, arithmetic and copies ran while one was open for 0% of the time, Pallas kernels for 8%

commit v1 on v0

--- a/solution.py
+++ b/solution.py
@@ -117,7 +117,7 @@
     return (control, increment)
 
 
-CHAIN = (4, 2, 1)
+CHAIN = (4, 2)
 UNROLL_PAIRS = 8
 UNROLL_MEMBERS = 16
 UNROLL_SUM = 16
@@ -398,7 +398,8 @@
             weighted = weight_ref[first_weight + member] * ens[block][member]
             return total + weighted * mapped[pl.ds(start, lev_dev), lanes]
 
-        image_ref[place ^ block] = lax.fori_loop(
+        half = len(ens) // 2
+        image_ref[(1 - block % 2) * half + (place ^ block) // 2] = lax.fori_loop(
             0, members, add, jnp.zeros((lev_dev, size), jnp.float32), unroll=UNROLL_SUM
         )
 
@@ -428,10 +429,11 @@
     members = ens[0].shape[0] - 2
     place = lax.axis_index("wide")
     total = jnp.zeros(image_ref.shape, jnp.float32)
-    for block, ens_ref in enumerate(ens):
-        image = one_ref[place ^ block] + two_ref[place ^ block]
+    for at, ens_ref in enumerate(ens):
+        block = (place ^ (2 * at)) // 2
+        image = one_ref[block] + two_ref[block]
         total = total + ens_ref[members + 1] * image * image
-        if block == 0:
+        if at == 0:
             image_ref[...] = image
     sums_ref[0] = one_ref[len(ens)] + two_ref[len(ens)]
     sums_ref[1] = total
@@ -538,18 +540,24 @@
     for other in range(1, wide):
         grads[other] = swap(grads[other], "wide", other)
     image = image_part(member_weight, taps, high, low, field, arrived)
+    half = wide // 2
+    kept = image[half:wide] + swap(image[:half], "wide", 1)
+    image = jnp.concatenate([kept, image[wide:]], axis=0)
     other_image = jnp.zeros_like(image)
     for step, other in enumerate(CHAIN):
         if step:
             image = image + other_image
         other_image = swap(image, "wide", other)
-    image, sums = observe(image, other_image, arrived)
-    step, other, other_sums = len(CHAIN), 1, jnp.zeros_like(sums)
-    while other < lax.axis_size("lev"):
-        if other > 1:
+    image, sums = observe(image, other_image, arrived[::2])
+    steps = [("wide", 1)]
+    while 1 << (len(steps) - 1) < lax.axis_size("lev"):
+        steps.append(("lev", 1 << (len(steps) - 1)))
+    steps = [steps[0], *steps[:0:-1]]
+    other_sums = jnp.zeros_like(sums)
+    for step, (axis, other) in enumerate(steps):
+        if step:
             sums = sums + other_sums
-        other_sums = swap(sums, "lev", other)
-        step, other = step + 1, other * 2
+        other_sums = swap(sums, axis, other)
     control, increment = finish(image, sums, other_sums, grads)
     return control.reshape(ensemble.shape), increment
 

time: 97.3 us -> 96.2 us (0.989)
  the two profiles are of different devices: /device:TPU:18 before, /device:TPU:0 now
where the time goes in v1:
time: 96.2 us; the launch traced here: 94.3 us
  starting transfers between devices  39.2 us (41%)
  waiting for transfers between devices  37.6 us (39%)
  Pallas kernels  16 us (17%)
  between operations  0.97 us (1%)
    ppermute x20, waiting for transfers between devices, swap(): return lax.ppermute(values, axes, [(i, i ^ other) for i in range(count)])  37.6 us
    ppermute x20, starting transfers between devices, swap(): return lax.ppermute(values, axes, [(i, i ^ other) for i in range(count)])  30.9 us
    ppermute x6, starting transfers between devices, halos(): received.append(lax.ppermute(edges, 'lev', pairs))  8.3 us
    pallas_call x3, Pallas kernels, gradient_part(): pl.pallas_call(functools.partial(gradient_kernel, begin, sofar is None),...  6.56 us
    pallas_call x1, Pallas kernels, image_part(): pl.pallas_call(image_kernel, out_shape=jax.ShapeDtypeStruct((len(arrived)...  3.47 us
    pallas_call x1, Pallas kernels, prepare(): pl.pallas_call(prepare_kernel, out_shape=(part, part, taps), in_specs=[IN...  2.73 us
  transfers between devices with their start and end apart: 26, of which 10 were waited for; matrix products, arithmetic and copies ran while one was open for 0% of the time, Pallas kernels for 8%

profile of v1, /device:TPU:0, one launch (start us, length us, event | category | flops | bytes accessed | tf_op | source)
XLA Modules:
  0.0 94.3 jit_solution(5350058681620127113)
XLA Ops:
  0.6 1.4 %shard_map.96 = (f32[18,16,128]{2,1,0:T(8,128)S(1)}, f32[18,16,128]{2,1,0:T(8,128)S(1)}, f32[18,16,128]{2,1,0:T(8,128)S(1)}, f32[18,16,128]{2,1,0:T(8,128)S(1)},...) custom-call(f32[8,16,16,128]{3,2,1,0:T(8,128)} %bitcast.35, ...), custom_call_target="tpu_custom_call" | custom-call | bytes 2097152 | tf_op jit(solution)/shard_map/pallas_call | solution.py:187
  2.1 4.1 %collective-permute-start = (f32[18,16,128]{2,1,0:T(8,128)S(1)}, f32[18,16,128]{2,1,0:T(8,128)S(1)}, u32[]{:S(2)}, u32[]{:S(2)}) collective-permute-start(f32[18,16,128]{2,1,0:T(8,128)S(1)} %get-tuple-element.29), channel_id=1, source_target_pairs={{0,16},{4,20},{8,24},{12,28},{16,0},{20,4},{24,8},{28,12},{1,17},{... | collective-permute-start | bytes 442376 | tf_op jit(solution)/shard_map/ppermute | solution.py:498
  6.2 1.3 %collective-permute-start.1 = (f32[18,16,128]{2,1,0:T(8,128)S(1)}, f32[18,16,128]{2,1,0:T(8,128)S(1)}, u32[]{:S(2)}, u32[]{:S(2)}) collective-permute-start(f32[18,16,128]{2,1,0:T(8,128)S(1)} %get-tuple-element.30), channel_id=1, source_target_pairs={{0,20},{4,16},{8,28},{12,24},{16,4},{20,0},{24,12},{28,8},{1,21},{... | collective-permute-start | bytes 442376 | tf_op jit(solution)/shard_map/ppermute | solution.py:498
  7.5 3.6 %collective-permute-start.4 = (f32[18,16,128]{2,1,0:T(8,128)S(1)}, f32[18,16,128]{2,1,0:T(8,128)S(1)}, u32[]{:S(2)}, u32[]{:S(2)}) collective-permute-start(f32[18,16,128]{2,1,0:T(8,128)S(1)} %get-tuple-element.31), channel_id=1, source_target_pairs={{0,24},{4,28},{8,16},{12,20},{16,8},{20,12},{24,0},{28,4},{1,25},{... | collective-permute-start | bytes 442376 | tf_op jit(solution)/shard_map/ppermute | solution.py:498
  11.1 1.7 %collective-permute-start.8 = (f32[18,16,128]{2,1,0:T(8,128)S(1)}, f32[18,16,128]{2,1,0:T(8,128)S(1)}, u32[]{:S(2)}, u32[]{:S(2)}) collective-permute-start(f32[18,16,128]{2,1,0:T(8,128)S(1)} %get-tuple-element.34), channel_id=1, source_target_pairs={{0,4},{4,0},{8,12},{12,8},{16,20},{20,16},{24,28},{28,24},{1,5},{5... | collective-permute-start | bytes 442376 | tf_op jit(solution)/shard_map/ppermute | solution.py:498
  12.9 2.7 %shard_map.95 = (bf16[1024,1024]{1,0:T(8,128)(2,1)S(1)}, bf16[1024,1024]{1,0:T(8,128)(2,1)S(1)}, f32[18,24,128]{2,1,0:T(8,128)S(1)}) custom-call(s32[8,8]{1,0:T(8,128)} %col_any.1, f32[8,128,128]{2,1,0:T(8,128)} %tiles_any.1, f32[80,128]{1,0:T(8,128)S(1)} %pad.4.weight_ref), custom_call_target="tpu_custom_call" | custom-call | flops 8388608 | bytes 8388608 | tf_op jit(solution)/shard_map/pallas_call | solution.py:257
  15.7 7.9 %collective-permute-done.refs_0_.refs_4_.refs_2_ = f32[18,16,128]{2,1,0:T(8,128)S(1)} collective-permute-done((f32[18,16,128]{2,1,0:T(8,128)S(1)}, f32[18,16,128]{2,1,0:T(8,128)S(1)}, u32[]{:S(2)}, u32[]{:S(2)}) %collective-permute-start) | collective-permute-done | bytes 147488 | tf_op jit(solution)/shard_map/ppermute | solution.py:498
  23.6 4.4 %collective-permute-done.1.refs_1_.refs_5_ = f32[18,16,128]{2,1,0:T(8,128)S(1)} collective-permute-done((f32[18,16,128]{2,1,0:T(8,128)S(1)}, f32[18,16,128]{2,1,0:T(8,128)S(1)}, u32[]{:S(2)}, u32[]{:S(2)}) %collective-permute-start.1) | collective-permute-done | bytes 147488 | tf_op jit(solution)/shard_map/ppermute | solution.py:498
  29.4 4.5 %collective-permute-done.10.refs_3_ = f32[18,16,128]{2,1,0:T(8,128)S(1)} collective-permute-done((f32[18,16,128]{2,1,0:T(8,128)S(1)}, f32[18,16,128]{2,1,0:T(8,128)S(1)}, u32[]{:S(2)}, u32[]{:S(2)}) %collective-permute-start.10) | collective-permute-done | bytes 147488 | tf_op jit(solution)/shard_map/ppermute | solution.py:498
  34.1 0.7 collective-permute-start.11
  34.8 2.9 %collective-permute-start.12 = (f32[4,17,8,128]{3,2,1,0:T(8,128)S(1)}, f32[4,17,8,128]{3,2,1,0:T(8,128)S(1)}, u32[]{:S(2)}, u32[]{:S(2)}) collective-permute-start(f32[4,17,8,128]{3,2,1,0:T(8,128)S(1)} %pad_maximum_fusion.1), channel_id=1, source_target_pairs={{0,1},{2,3},{1,0},{3,2},{4,5},{6,7},{5,4},{7,6},{8,9},{10,11},{9,8... | collective-permute-start | bytes 835592 | tf_op jit(solution)/shard_map/ppermute | solution.py:513
  38.4 1.3 %collective-permute-start.7 = (f32[2,17,8,128]{3,2,1,0:T(8,128)S(1)}, f32[2,17,8,128]{3,2,1,0:T(8,128)S(1)}, u32[]{:S(2)}, u32[]{:S(2)}) collective-permute-start(f32[2,17,8,128]{3,2,1,0:T(8,128)S(1)} %pad_maximum_fusion.5), channel_id=1, source_target_pairs={{0,1},{2,3},{1,0},{3,2},{4,5},{6,7},{5,4},{7,6},{8,9},{10,11},{9,8... | collective-permute-start | bytes 417800 | tf_op jit(solution)/shard_map/ppermute | solution.py:513
  39.8 2.1 %collective-permute-start.3 = (f32[2,17,8,128]{3,2,1,0:T(8,128)S(1)}, f32[2,17,8,128]{3,2,1,0:T(8,128)S(1)}, u32[]{:S(2)}, u32[]{:S(2)}) collective-permute-start(f32[2,17,8,128]{3,2,1,0:T(8,128)S(1)} %pad_maximum_fusion.3), channel_id=1, source_target_pairs={{0,1},{2,3},{1,0},{3,2},{4,5},{6,7},{5,4},{7,6},{8,9},{10,11},{9,8... | collective-permute-start | bytes 417800 | tf_op jit(solution)/shard_map/ppermute | solution.py:513
  41.8 2.9 %shard_map.97.refs_2_ = f32[384,1024]{1,0:T(8,128)S(1)} custom-call(f32[128]{0:T(128)S(1)} %copy-done, f32[18,24,128]{2,1,0:T(8,128)S(1)} %get-tuple-element.26.taps_ref, bf16[1024,1024]{1,0:T(8,128)(2,1)S(1)} %get-tuple-element.27.high, bf16[1024,1024]{1,0:T(8,128)(2,1)S(1)} %get-tuple-element.28.low, f32[4,17,8,128]{3,2,1,0:T(8,128)S(1)} %collective-permute-done.11.far, ...), custom_call_target="tpu_custom_call" | custom-call | flops 1207959552 | bytes 1572864 | tf_op jit(solution)/shard_map/pallas_call | solution.py:350
  44.7 1.8 %shard_map.98.refs_2_ = f32[384,1024]{1,0:T(8,128)S(1)} custom-call(f32[128]{0:T(128)S(1)} %copy-done, f32[18,24,128]{2,1,0:T(8,128)S(1)} %get-tuple-element.26.taps_ref, bf16[1024,1024]{1,0:T(8,128)(2,1)S(1)} %get-tuple-element.27.high, bf16[1024,1024]{1,0:T(8,128)(2,1)S(1)} %get-tuple-element.28.low, f32[2,17,8,128]{3,2,1,0:T(8,128)S(1)} %collective-permute-done.6.far, ...), custom_call_target="tpu_custom_call" | custom-call | flops 603979776 | bytes 1572864 | tf_op jit(solution)/shard_map/pallas_call | solution.py:350
  46.5 1.9 %shard_map.99 = (f32[384,1024]{1,0:T(8,128)S(1)}, f32[16,16,128]{2,1,0:T(8,128)S(1)}, f32[16,16,128]{2,1,0:T(8,128)S(1)}, f32[16,16,128]{2,1,0:T(8,128)S(1)}, f3...) custom-call(f32[128]{0:T(128)S(1)} %copy-done, ...), custom_call_target="tpu_custom_call" | custom-call | flops 603979776 | bytes 1572864 | tf_op jit(solution)/shard_map/pallas_call | solution.py:350
  48.4 3.5 %shard_map.100 = f32[9,16,128]{2,1,0:T(8,128)S(1)} custom-call(f32[128]{0:T(128)S(1)} %copy-done, f32[18,24,128]{2,1,0:T(8,128)S(1)} %get-tuple-element.26.taps_ref, bf16[1024,1024]{1,0:T(8,128)(2,1)S(1)} %get-tuple-element.27.high, bf16[1024,1024]{1,0:T(8,128)(2,1)S(1)} %get-tuple-element.28.low, f32[384,1024]{1,0:T(8,128)S(1)} %get-tuple-element.37.field, ...), custom_call_target="tpu_custom_call" | custom-call | flops 1610612736 | bytes 1048576 | tf_op jit(solution)/shard_map/pallas_call | solution.py:411
  52.5 3.4 %collective-permute-done.13 = f32[4,16,128]{2,1,0:T(8,128)S(1)} collective-permute-done((f32[4,16,128]{2,1,0:T(8,128)S(1)}, f32[4,16,128]{2,1,0:T(8,128)S(1)}, u32[]{:S(2)}, u32[]{:S(2)}) %collective-permute-start.13) | collective-permute-done | bytes 32800 | tf_op jit(solution)/shard_map/ppermute | solution.py:498
  55.9 4.3 %collective-permute-start.14 = (f32[5,16,128]{2,1,0:T(8,128)S(1)}, f32[5,16,128]{2,1,0:T(8,128)S(1)}, u32[]{:S(2)}, u32[]{:S(2)}) collective-permute-start(f32[5,16,128]{2,1,0:T(8,128)S(1)} %pad_maximum_fusion.6), channel_id=1, source_target_pairs={{0,16},{4,20},{8,24},{12,28},{16,0},{20,4},{24,8},{28,12},{1,17},{... | collective-permute-start | bytes 122888 | tf_op jit(solution)/shard_map/ppermute | solution.py:498
  60.2 1.2 %collective-permute-start.19 = (f32[16,16,128]{2,1,0:T(8,128)S(1)}, f32[16,16,128]{2,1,0:T(8,128)S(1)}, u32[]{:S(2)}, u32[]{:S(2)}) collective-permute-start(f32[16,16,128]{2,1,0:T(8,128)S(1)} %get-tuple-element.41), channel_id=1, source_target_pairs={{0,4},{4,0},{8,12},{12,8},{16,20},{20,16},{24,28},{28,24},{1,5},{5... | collective-permute-start | bytes 393224 | tf_op jit(solution)/shard_map/ppermute | solution.py:498
  61.5 0.8 collective-permute-done.14
  62.3 1.3 %collective-permute-start.15 = (f32[5,16,128]{2,1,0:T(8,128)S(1)}, f32[5,16,128]{2,1,0:T(8,128)S(1)}, u32[]{:S(2)}, u32[]{:S(2)}) collective-permute-start(f32[5,16,128]{2,1,0:T(8,128)S(1)} %fusion.one_ref), channel_id=1, source_target_pairs={{0,8},{4,12},{8,0},{12,4},{16,24},{20,28},{24,16},{28,20},{1,9},{5... | collective-permute-start | bytes 122888 | tf_op jit(solution)/shard_map/ppermute | solution.py:498
  63.6 3.3 %collective-permute-done.15.two_ref = f32[5,16,128]{2,1,0:T(8,128)S(1)} collective-permute-done((f32[5,16,128]{2,1,0:T(8,128)S(1)}, f32[5,16,128]{2,1,0:T(8,128)S(1)}, u32[]{:S(2)}, u32[]{:S(2)}) %collective-permute-start.15) | collective-permute-done | bytes 40992 | tf_op jit(solution)/shard_map/ppermute | solution.py:498
  66.9 1.2 %collective-permute-start.16 = (f32[2,16,128]{2,1,0:T(8,128)S(1)}, f32[2,16,128]{2,1,0:T(8,128)S(1)}, u32[]{:S(2)}, u32[]{:S(2)}) collective-permute-start(f32[2,16,128]{2,1,0:T(8,128)S(1)} %get-tuple-element.39), channel_id=1, source_target_pairs={{0,4},{4,0},{8,12},{12,8},{16,20},{20,16},{24,28},{28,24},{1,5},{5... | collective-permute-start | bytes 49160 | tf_op jit(solution)/shard_map/ppermute | solution.py:498
  68.1 2.6 %collective-permute-done.16 = f32[2,16,128]{2,1,0:T(8,128)S(1)} collective-permute-done((f32[2,16,128]{2,1,0:T(8,128)S(1)}, f32[2,16,128]{2,1,0:T(8,128)S(1)}, u32[]{:S(2)}, u32[]{:S(2)}) %collective-permute-start.16) | collective-permute-done | bytes 16416 | tf_op jit(solution)/shard_map/ppermute | solution.py:498
  70.7 1.6 %collective-permute-start.17 = (f32[2,16,128]{2,1,0:T(8,128)S(1)}, f32[2,16,128]{2,1,0:T(8,128)S(1)}, u32[]{:S(2)}, u32[]{:S(2)}) collective-permute-start(f32[2,16,128]{2,1,0:T(8,128)S(1)} %add.45), channel_id=1, source_target_pairs={{0,2},{1,3},{2,0},{3,1},{4,6},{5,7},{6,4},{7,5},{8,10},{9,11},{10,... | collective-permute-start | bytes 49160 | tf_op jit(solution)/shard_map/ppermute | solution.py:498
  72.3 1.0 %collective-permute-start.21 = (f32[16,16,128]{2,1,0:T(8,128)S(1)}, f32[16,16,128]{2,1,0:T(8,128)S(1)}, u32[]{:S(2)}, u32[]{:S(2)}) collective-permute-start(f32[16,16,128]{2,1,0:T(8,128)S(1)} %get-tuple-element.43), channel_id=1, source_target_pairs={{0,12},{4,8},{8,4},{12,0},{16,28},{20,24},{24,20},{28,16},{1,13},{... | collective-permute-start | bytes 393224 | tf_op jit(solution)/shard_map/ppermute | solution.py:498
  73.3 3.2 %collective-permute-start.22 = (f32[16,16,128]{2,1,0:T(8,128)S(1)}, f32[16,16,128]{2,1,0:T(8,128)S(1)}, u32[]{:S(2)}, u32[]{:S(2)}) collective-permute-start(f32[16,16,128]{2,1,0:T(8,128)S(1)} %get-tuple-element.44), channel_id=1, source_target_pairs={{0,16},{4,20},{8,24},{12,28},{16,0},{20,4},{24,8},{28,12},{1,17},{... | collective-permute-start | bytes 393224 | tf_op jit(solution)/shard_map/ppermute | solution.py:498
  77.0 4.8 %collective-permute-start.24 = (f32[16,16,128]{2,1,0:T(8,128)S(1)}, f32[16,16,128]{2,1,0:T(8,128)S(1)}, u32[]{:S(2)}, u32[]{:S(2)}) collective-permute-start(f32[16,16,128]{2,1,0:T(8,128)S(1)} %get-tuple-element.46), channel_id=1, source_target_pairs={{0,24},{4,28},{8,16},{12,20},{16,8},{20,12},{24,0},{28,4},{1,25},{... | collective-permute-start | bytes 393224 | tf_op jit(solution)/shard_map/ppermute | solution.py:498
  82.3 6.8 %collective-permute-done.22.refs_6_ = f32[16,16,128]{2,1,0:T(8,128)S(1)} collective-permute-done((f32[16,16,128]{2,1,0:T(8,128)S(1)}, f32[16,16,128]{2,1,0:T(8,128)S(1)}, u32[]{:S(2)}, u32[]{:S(2)}) %collective-permute-start.22) | collective-permute-done | bytes 131104 | tf_op jit(solution)/shard_map/ppermute | solution.py:498
  89.2 3.3 %collective-permute-done.23.refs_7_ = f32[16,16,128]{2,1,0:T(8,128)S(1)} collective-permute-done((f32[16,16,128]{2,1,0:T(8,128)S(1)}, f32[16,16,128]{2,1,0:T(8,128)S(1)}, u32[]{:S(2)}, u32[]{:S(2)}) %collective-permute-start.23) | collective-permute-done | bytes 131104 | tf_op jit(solution)/shard_map/ppermute | solution.py:498
  92.5 1.8 %shard_map.102 = (f32[8,16,16,128]{3,2,1,0:T(8,128)}, f32[16,128]{1,0:T(8,128)}) custom-call(f32[16,128]{1,0:T(8,128)S(1)} %get-tuple-element.38.image_ref, f32[2,16,128]{2,1,0:T(8,128)S(1)} %add.46.refs_0_, f32[2,16,128]{2,1,0:T(8,128)S(1)} %collective-permute-done.18.refs_1_, f32[16,16,128]{2,1,0:T(8,128)S(1)} %get-tuple-element.40.refs_2_, ...), custom_call_target="tpu_custom_call" | custom-call | tf_op jit(solution)/shard_map/pallas_call | solution.py:483
  (63 shorter events, 4.1 us)
Async XLA Ops:
  0.6 12.2 %copy-start.1 = (f32[9,64]{1,0:T(8,128)S(1)}, f32[9,64]{1,0:T(8,128)}, u32[]{:S(2)}) copy-start(f32[9,64]{1,0:T(8,128)} %param.13) | copy-start | bytes 6916
  2.1 21.5 %collective-permute-start = (f32[18,16,128]{2,1,0:T(8,128)S(1)}, f32[18,16,128]{2,1,0:T(8,128)S(1)}, u32[]{:S(2)}, u32[]{:S(2)}) collective-permute-start(f32[18,16,128]{2,1,0:T(8,128)S(1)} %get-tuple-element.29), channel_id=1, source_target_pairs={{0,16},{4,20},{8,24},{12,28},{16,0},{20,4},{24,8},{28,12},{1,17},{... | collective-permute-start | bytes 442376 | tf_op jit(solution)/shard_map/ppermute | solution.py:498
  6.2 21.8 %collective-permute-start.1 = (f32[18,16,128]{2,1,0:T(8,128)S(1)}, f32[18,16,128]{2,1,0:T(8,128)S(1)}, u32[]{:S(2)}, u32[]{:S(2)}) collective-permute-start(f32[18,16,128]{2,1,0:T(8,128)S(1)} %get-tuple-element.30), channel_id=1, source_target_pairs={{0,20},{4,16},{8,28},{12,24},{16,4},{20,0},{24,12},{28,8},{1,21},{... | collective-permute-start | bytes 442376 | tf_op jit(solution)/shard_map/ppermute | solution.py:498
  7.5 20.5 %collective-permute-start.4 = (f32[18,16,128]{2,1,0:T(8,128)S(1)}, f32[18,16,128]{2,1,0:T(8,128)S(1)}, u32[]{:S(2)}, u32[]{:S(2)}) collective-permute-start(f32[18,16,128]{2,1,0:T(8,128)S(1)} %get-tuple-element.31), channel_id=1, source_target_pairs={{0,24},{4,28},{8,16},{12,20},{16,8},{20,12},{24,0},{28,4},{1,25},{... | collective-permute-start | bytes 442376 | tf_op jit(solution)/shard_map/ppermute | solution.py:498
  11.1 17.7 %collective-permute-start.5 = (f32[18,16,128]{2,1,0:T(8,128)S(1)}, f32[18,16,128]{2,1,0:T(8,128)S(1)}, u32[]{:S(2)}, u32[]{:S(2)}) collective-permute-start(f32[18,16,128]{2,1,0:T(8,128)S(1)} %get-tuple-element.32), channel_id=1, source_target_pairs={{0,28},{4,24},{8,20},{12,16},{16,12},{20,8},{24,4},{28,0},{1,29},{... | collective-permute-start | bytes 442376 | tf_op jit(solution)/shard_map/ppermute | solution.py:498
  11.1 17.7 %collective-permute-start.8 = (f32[18,16,128]{2,1,0:T(8,128)S(1)}, f32[18,16,128]{2,1,0:T(8,128)S(1)}, u32[]{:S(2)}, u32[]{:S(2)}) collective-permute-start(f32[18,16,128]{2,1,0:T(8,128)S(1)} %get-tuple-element.34), channel_id=1, source_target_pairs={{0,4},{4,0},{8,12},{12,8},{16,20},{20,16},{24,28},{28,24},{1,5},{5... | collective-permute-start | bytes 442376 | tf_op jit(solution)/shard_map/ppermute | solution.py:498
  23.5 5.9 %collective-permute-start.9 = (f32[18,16,128]{2,1,0:T(8,128)S(1)}, f32[18,16,128]{2,1,0:T(8,128)S(1)}, u32[]{:S(2)}, u32[]{:S(2)}) collective-permute-start(f32[18,16,128]{2,1,0:T(8,128)S(1)} %get-tuple-element.35), channel_id=1, source_target_pairs={{0,8},{4,12},{8,0},{12,4},{16,24},{20,28},{24,16},{28,20},{1,9},{5... | collective-permute-start | bytes 442376 | tf_op jit(solution)/shard_map/ppermute | solution.py:498
  28.0 6.0 %collective-permute-start.10 = (f32[18,16,128]{2,1,0:T(8,128)S(1)}, f32[18,16,128]{2,1,0:T(8,128)S(1)}, u32[]{:S(2)}, u32[]{:S(2)}) collective-permute-start(f32[18,16,128]{2,1,0:T(8,128)S(1)} %get-tuple-element.36), channel_id=1, source_target_pairs={{0,12},{4,8},{8,4},{12,0},{16,28},{20,24},{24,20},{28,16},{1,13},{... | collective-permute-start | bytes 442376 | tf_op jit(solution)/shard_map/ppermute | solution.py:498
  28.0 18.5 %collective-permute-start.2 = (f32[2,17,8,128]{3,2,1,0:T(8,128)S(1)}, f32[2,17,8,128]{3,2,1,0:T(8,128)S(1)}, u32[]{:S(2)}, u32[]{:S(2)}) collective-permute-start(f32[2,17,8,128]{3,2,1,0:T(8,128)S(1)} %pad_maximum_fusion.2), channel_id=1, source_target_pairs={{1,2},{2,1},{5,6},{6,5},{9,10},{10,9},{13,14},{14,13},{17,18},{18,... | collective-permute-start | bytes 417800 | tf_op jit(solution)/shard_map/ppermute | solution.py:513
  28.9 12.9 %copy-start = (f32[128]{0:T(128)S(1)}, f32[128]{0:T(128)}, u32[]{:S(2)}) copy-start(f32[128]{0:T(128)} %weight_ref.7) | copy-start | bytes 1540
  34.1 5.7 %collective-permute-start.11 = (f32[4,17,8,128]{3,2,1,0:T(8,128)S(1)}, f32[4,17,8,128]{3,2,1,0:T(8,128)S(1)}, u32[]{:S(2)}, u32[]{:S(2)}) collective-permute-start(f32[4,17,8,128]{3,2,1,0:T(8,128)S(1)} %pad_maximum_fusion), channel_id=1, source_target_pairs={{1,2},{2,1},{5,6},{6,5},{9,10},{10,9},{13,14},{14,13},{17,18},{18,... | collective-permute-start | bytes 835592 | tf_op jit(solution)/shard_map/ppermute | solution.py:513
  34.8 7.0 %collective-permute-start.12 = (f32[4,17,8,128]{3,2,1,0:T(8,128)S(1)}, f32[4,17,8,128]{3,2,1,0:T(8,128)S(1)}, u32[]{:S(2)}, u32[]{:S(2)}) collective-permute-start(f32[4,17,8,128]{3,2,1,0:T(8,128)S(1)} %pad_maximum_fusion.1), channel_id=1, source_target_pairs={{0,1},{2,3},{1,0},{3,2},{4,5},{6,7},{5,4},{7,6},{8,9},{10,11},{9,8... | collective-permute-start | bytes 835592 | tf_op jit(solution)/shard_map/ppermute | solution.py:513
  37.7 7.0 %collective-permute-start.6 = (f32[2,17,8,128]{3,2,1,0:T(8,128)S(1)}, f32[2,17,8,128]{3,2,1,0:T(8,128)S(1)}, u32[]{:S(2)}, u32[]{:S(2)}) collective-permute-start(f32[2,17,8,128]{3,2,1,0:T(8,128)S(1)} %pad_maximum_fusion.4), channel_id=1, source_target_pairs={{1,2},{2,1},{5,6},{6,5},{9,10},{10,9},{13,14},{14,13},{17,18},{18,... | collective-permute-start | bytes 417800 | tf_op jit(solution)/shard_map/ppermute | solution.py:513
  38.4 6.3 %collective-permute-start.7 = (f32[2,17,8,128]{3,2,1,0:T(8,128)S(1)}, f32[2,17,8,128]{3,2,1,0:T(8,128)S(1)}, u32[]{:S(2)}, u32[]{:S(2)}) collective-permute-start(f32[2,17,8,128]{3,2,1,0:T(8,128)S(1)} %pad_maximum_fusion.5), channel_id=1, source_target_pairs={{0,1},{2,3},{1,0},{3,2},{4,5},{6,7},{5,4},{7,6},{8,9},{10,11},{9,8... | collective-permute-start | bytes 417800 | tf_op jit(solution)/shard_map/ppermute | solution.py:513
  39.8 6.8 %collective-permute-start.3 = (f32[2,17,8,128]{3,2,1,0:T(8,128)S(1)}, f32[2,17,8,128]{3,2,1,0:T(8,128)S(1)}, u32[]{:S(2)}, u32[]{:S(2)}) collective-permute-start(f32[2,17,8,128]{3,2,1,0:T(8,128)S(1)} %pad_maximum_fusion.3), channel_id=1, source_target_pairs={{0,1},{2,3},{1,0},{3,2},{4,5},{6,7},{5,4},{7,6},{8,9},{10,11},{9,8... | collective-permute-start | bytes 417800 | tf_op jit(solution)/shard_map/ppermute | solution.py:513
  51.9 4.0 %collective-permute-start.13 = (f32[4,16,128]{2,1,0:T(8,128)S(1)}, f32[4,16,128]{2,1,0:T(8,128)S(1)}, u32[]{:S(2)}, u32[]{:S(2)}) collective-permute-start(f32[4,16,128]{2,1,0:T(8,128)S(1)} %slice.60), channel_id=1, source_target_pairs={{0,4},{4,0},{8,12},{12,8},{16,20},{20,16},{24,28},{28,24},{1,5},{5... | collective-permute-start | bytes 98312 | tf_op jit(solution)/shard_map/ppermute | solution.py:498
  55.9 6.4 %collective-permute-start.14 = (f32[5,16,128]{2,1,0:T(8,128)S(1)}, f32[5,16,128]{2,1,0:T(8,128)S(1)}, u32[]{:S(2)}, u32[]{:S(2)}) collective-permute-start(f32[5,16,128]{2,1,0:T(8,128)S(1)} %pad_maximum_fusion.6), channel_id=1, source_target_pairs={{0,16},{4,20},{8,24},{12,28},{16,0},{20,4},{24,8},{28,12},{1,17},{... | collective-permute-start | bytes 122888 | tf_op jit(solution)/shard_map/ppermute | solution.py:498
  60.2 16.2 %collective-permute-start.19 = (f32[16,16,128]{2,1,0:T(8,128)S(1)}, f32[16,16,128]{2,1,0:T(8,128)S(1)}, u32[]{:S(2)}, u32[]{:S(2)}) collective-permute-start(f32[16,16,128]{2,1,0:T(8,128)S(1)} %get-tuple-element.41), channel_id=1, source_target_pairs={{0,4},{4,0},{8,12},{12,8},{16,20},{20,16},{24,28},{28,24},{1,5},{5... | collective-permute-start | bytes 393224 | tf_op jit(solution)/shard_map/ppermute | solution.py:498
  61.5 15.5 %collective-permute-start.20 = (f32[16,16,128]{2,1,0:T(8,128)S(1)}, f32[16,16,128]{2,1,0:T(8,128)S(1)}, u32[]{:S(2)}, u32[]{:S(2)}) collective-permute-start(f32[16,16,128]{2,1,0:T(8,128)S(1)} %get-tuple-element.42), channel_id=1, source_target_pairs={{0,8},{4,12},{8,0},{12,4},{16,24},{20,28},{24,16},{28,20},{1,9},{5... | collective-permute-start | bytes 393224 | tf_op jit(solution)/shard_map/ppermute | solution.py:498
  62.3 4.6 %collective-permute-start.15 = (f32[5,16,128]{2,1,0:T(8,128)S(1)}, f32[5,16,128]{2,1,0:T(8,128)S(1)}, u32[]{:S(2)}, u32[]{:S(2)}) collective-permute-start(f32[5,16,128]{2,1,0:T(8,128)S(1)} %fusion.one_ref), channel_id=1, source_target_pairs={{0,8},{4,12},{8,0},{12,4},{16,24},{20,28},{24,16},{28,20},{1,9},{5... | collective-permute-start | bytes 122888 | tf_op jit(solution)/shard_map/ppermute | solution.py:498
  66.9 3.8 %collective-permute-start.16 = (f32[2,16,128]{2,1,0:T(8,128)S(1)}, f32[2,16,128]{2,1,0:T(8,128)S(1)}, u32[]{:S(2)}, u32[]{:S(2)}) collective-permute-start(f32[2,16,128]{2,1,0:T(8,128)S(1)} %get-tuple-element.39), channel_id=1, source_target_pairs={{0,4},{4,0},{8,12},{12,8},{16,20},{20,16},{24,28},{28,24},{1,5},{5... | collective-permute-start | bytes 49160 | tf_op jit(solution)/shard_map/ppermute | solution.py:498
  70.7 11.1 %collective-permute-start.17 = (f32[2,16,128]{2,1,0:T(8,128)S(1)}, f32[2,16,128]{2,1,0:T(8,128)S(1)}, u32[]{:S(2)}, u32[]{:S(2)}) collective-permute-start(f32[2,16,128]{2,1,0:T(8,128)S(1)} %add.45), channel_id=1, source_target_pairs={{0,2},{1,3},{2,0},{3,1},{4,6},{5,7},{6,4},{7,5},{8,10},{9,11},{10,... | collective-permute-start | bytes 49160 | tf_op jit(solution)/shard_map/ppermute | solution.py:498
  72.3 9.9 %collective-permute-start.21 = (f32[16,16,128]{2,1,0:T(8,128)S(1)}, f32[16,16,128]{2,1,0:T(8,128)S(1)}, u32[]{:S(2)}, u32[]{:S(2)}) collective-permute-start(f32[16,16,128]{2,1,0:T(8,128)S(1)} %get-tuple-element.43), channel_id=1, source_target_pairs={{0,12},{4,8},{8,4},{12,0},{16,28},{20,24},{24,20},{28,16},{1,13},{... | collective-permute-start | bytes 393224 | tf_op jit(solution)/shard_map/ppermute | solution.py:498
  73.3 15.9 %collective-permute-start.22 = (f32[16,16,128]{2,1,0:T(8,128)S(1)}, f32[16,16,128]{2,1,0:T(8,128)S(1)}, u32[]{:S(2)}, u32[]{:S(2)}) collective-permute-start(f32[16,16,128]{2,1,0:T(8,128)S(1)} %get-tuple-element.44), channel_id=1, source_target_pairs={{0,16},{4,20},{8,24},{12,28},{16,0},{20,4},{24,8},{28,12},{1,17},{... | collective-permute-start | bytes 393224 | tf_op jit(solution)/shard_map/ppermute | solution.py:498
  76.5 16.0 %collective-permute-start.23 = (f32[16,16,128]{2,1,0:T(8,128)S(1)}, f32[16,16,128]{2,1,0:T(8,128)S(1)}, u32[]{:S(2)}, u32[]{:S(2)}) collective-permute-start(f32[16,16,128]{2,1,0:T(8,128)S(1)} %get-tuple-element.45), channel_id=1, source_target_pairs={{0,20},{4,16},{8,28},{12,24},{16,4},{20,0},{24,12},{28,8},{1,21},{... | collective-permute-start | bytes 393224 | tf_op jit(solution)/shard_map/ppermute | solution.py:498
  77.0 15.5 %collective-permute-start.24 = (f32[16,16,128]{2,1,0:T(8,128)S(1)}, f32[16,16,128]{2,1,0:T(8,128)S(1)}, u32[]{:S(2)}, u32[]{:S(2)}) collective-permute-start(f32[16,16,128]{2,1,0:T(8,128)S(1)} %get-tuple-element.46), channel_id=1, source_target_pairs={{0,24},{4,28},{8,16},{12,20},{16,8},{20,12},{24,0},{28,4},{1,25},{... | collective-permute-start | bytes 393224 | tf_op jit(solution)/shard_map/ppermute | solution.py:498
  81.8 10.7 %collective-permute-start.25 = (f32[16,16,128]{2,1,0:T(8,128)S(1)}, f32[16,16,128]{2,1,0:T(8,128)S(1)}, u32[]{:S(2)}, u32[]{:S(2)}) collective-permute-start(f32[16,16,128]{2,1,0:T(8,128)S(1)} %get-tuple-element.47), channel_id=1, source_target_pairs={{0,28},{4,24},{8,20},{12,16},{16,12},{20,8},{24,4},{28,0},{1,29},{... | collective-permute-start | bytes 393224 | tf_op jit(solution)/shard_map/ppermute | solution.py:498
  82.3 10.2 %collective-permute-start.18 = (f32[2,16,128]{2,1,0:T(8,128)S(1)}, f32[2,16,128]{2,1,0:T(8,128)S(1)}, u32[]{:S(2)}, u32[]{:S(2)}) collective-permute-start(f32[2,16,128]{2,1,0:T(8,128)S(1)} %add.46.refs_0_), channel_id=1, source_target_pairs={{0,1},{1,0},{2,3},{3,2},{4,5},{5,4},{6,7},{7,6},{8,9},{9,8},{10,11... | collective-permute-start | bytes 49160 | tf_op jit(solution)/shard_map/ppermute | solution.py:498
